TPU v7x, 32 devices: a whole 2x2x4 slice. The times are simulated.
32 devices in a mesh: dp: 4 (over y, core), expert: 8 (over z, x).
Axes of the slice: x: 2, y: 2, z: 4, core: 2. Of those that a mesh axis runs over, the one named last changes fastest.
Arguments:
- patches: bfloat16 [16384, 768], P(('dp', 'expert')), may hold values from -6 to 6
- owner_slot: int32 [128], P(('dp', 'expert')), may hold values from 0 to 127, as said below
- segment_ids: int32 [16384], P(('dp', 'expert')), may hold values from 0 to 127, as said below
- block_mask: int32 [128, 4], P(('dp', 'expert')), may hold values from 0 to 1, as said below
- project_in: bfloat16 [768, 2304], replicated, may hold values from -30 to 30
- project_out: bfloat16 [768, 768], replicated, may hold values from -0.21875 to 0.21875
- slot_keys: bfloat16 [768, 32], replicated, may hold values from -30 to 30
- expert_in: bfloat16 [32, 768, 3072], P(('dp', 'expert')), may hold values from -0.21875 to 0.21875
- expert_out: bfloat16 [32, 3072, 768], P(('dp', 'expert')), may hold values from -0.109375 to 0.109375
Outputs:
- layer_out: bfloat16 [16384, 768], P(('dp', 'expert'))
Inputs may be any that keep to these rules, and one draw needn't show every extreme that they name: A permutation of the 128 blocks. Devices are numbered over dp then expert, and block g is read by device g // 4; it goes to device owner_slot[g] // 4, which has the same index along expert. Each reading device sends exactly 1 block to each of 4 distinct devices along dp, and each device receives exactly 4 blocks. `segment_ids`: Non-decreasing; the rows of run o (rows o * 512 to o * 512 + 511) carry the image numbers o * 4 to o * 4 + 3, each on one row or more. block_mask[o * 4 + a, b] is 1 when blocks a and b of run o hold rows of a common image, else 0.
All inputs are finite; a program needn't handle non-finite values.
Results may differ from a plain program's by a relative error of at most 0.0095.
The roundings to bfloat16 on the way count: a program that leaves them out, or rounds other values in their place, can miss the bound.
Values may be sent and summed in bfloat16 or wider, within the bound.
No kernel may reach another device: no remote copies, remote signals or barrier semaphores. Data moves between devices by JAX's collectives and lax.ppermute only.
A program may use at most 128 MiB of HBM per device.

v0:
```python
import jax
import jax.numpy as jnp
from jax import lax
from jax.sharding import PartitionSpec as P

HEADS = 12
HEAD = 64
EPS = 1e-06
NEGATIVE = -1e30


def layer_norm(values):
    values = values.astype(jnp.float32)
    centred = values - jnp.mean(values, axis=-1, keepdims=True)
    variance = jnp.mean(centred * centred, axis=-1, keepdims=True)
    return centred * lax.rsqrt(variance + EPS)


def per_device(
    patches,
    owner_slot,
    segment_ids,
    block_mask,
    project_in,
    project_out,
    slot_keys,
    expert_in,
    expert_out,
):
    width = patches.shape[1]
    blk_count = owner_slot.shape[0]
    tok_count = patches.shape[0]
    block_rows = tok_count // blk_count
    data_count = lax.axis_size("dp")
    column_count = lax.axis_size("expert")
    peer_cap = max(1, blk_count // data_count)
    slot_total = data_count * peer_cap
    highest = lax.Precision.HIGHEST
    target_data = owner_slot // blk_count // column_count
    target_place = owner_slot % blk_count
    to_peer = (target_data[:, None] == jnp.arange(data_count, dtype=jnp.int32)[None, :]).astype(
        jnp.int32
    )
    peer_rank = jnp.sum((jnp.cumsum(to_peer, axis=0) - 1) * to_peer, axis=1)
    send_index = target_data * peer_cap + peer_rank
    route = send_index[None, :] == jnp.arange(slot_total, dtype=jnp.int32)[:, None]
    flat_blocks = patches.reshape(blk_count, block_rows * width)
    send_rows = jnp.dot(
        route.astype(jnp.bfloat16), flat_blocks, preferred_element_type=jnp.float32
    ).astype(jnp.bfloat16)
    send_place = jnp.sum(route.astype(jnp.int32) * (target_place[None, :] + 1), axis=1) - 1
    arrived_rows, arrived_place = (
        lax.all_to_all(
            send_rows.reshape(data_count, peer_cap, block_rows * width),
            "dp",
            split_axis=0,
            concat_axis=0,
            tiled=True,
        ),
        lax.all_to_all(
            send_place.reshape(data_count, peer_cap), "dp", split_axis=0, concat_axis=0, tiled=True
        ),
    )
    placing = (
        arrived_place.reshape(1, slot_total) == jnp.arange(blk_count, dtype=jnp.int32)[:, None]
    ).astype(jnp.bfloat16)
    ordered = jnp.dot(
        placing,
        arrived_rows.reshape(slot_total, block_rows * width),
        preferred_element_type=jnp.float32,
    )
    ordered = ordered.astype(jnp.bfloat16).reshape(tok_count, width)
    normed = layer_norm(ordered).astype(jnp.bfloat16)
    joint = jnp.dot(normed, project_in, preferred_element_type=jnp.float32).astype(jnp.bfloat16)
    queries = joint[:, :width].reshape(tok_count, HEADS, HEAD)
    key_rows = joint[:, width : 2 * width].reshape(tok_count, HEADS, HEAD)
    value_rows = joint[:, 2 * width :].reshape(tok_count, HEADS, HEAD)
    linked_blocks = jnp.broadcast_to(
        block_mask[:, None, :, None] == 1, (blk_count, block_rows, blk_count, block_rows)
    ).reshape(tok_count, tok_count)
    linked = linked_blocks & (segment_ids[:, None] == segment_ids[None, :])
    scores = jnp.einsum(
        "qhd,khd->hqk", queries, key_rows, preferred_element_type=jnp.float32
    ) * HEAD ** (-0.5)
    scores = jnp.where(linked[None], scores, NEGATIVE)
    raised = jnp.exp(scores - jnp.max(scores, axis=2, keepdims=True))
    weights = (raised / jnp.sum(raised, axis=2, keepdims=True)).astype(jnp.bfloat16)
    attended = jnp.einsum("hqk,khd->qhd", weights, value_rows, preferred_element_type=jnp.float32)
    pieces = attended.astype(jnp.bfloat16).reshape(-1, width)
    hidden = (
        ordered.astype(jnp.float32)
        + jnp.dot(pieces, project_out, preferred_element_type=jnp.float32)
    ).astype(jnp.bfloat16)
    moe_normed = layer_norm(hidden).astype(jnp.bfloat16)
    logits = jnp.dot(moe_normed, slot_keys, preferred_element_type=jnp.float32)
    local_image = segment_ids % blk_count
    member = local_image[None, :] == jnp.arange(blk_count, dtype=jnp.int32)[:, None]
    member_float = member.astype(jnp.float32)
    column_max = jnp.max(jnp.where(member[:, :, None], logits[None], NEGATIVE), axis=1)
    row_shift = jnp.dot(member_float.T, column_max, precision=highest)
    raised_slots = jnp.exp(logits - row_shift)
    totals = jnp.dot(member_float, raised_slots, precision=highest)
    row_totals = jnp.dot(member_float.T, totals, precision=highest)
    dispatch = (raised_slots / row_totals).astype(jnp.bfloat16)
    masked = jnp.where(member[:, :, None], dispatch[None], jnp.zeros((), jnp.bfloat16))
    slot_in = jnp.einsum(
        "ste,td->sed", masked, moe_normed, preferred_element_type=jnp.float32
    ).astype(jnp.bfloat16)
    slot_raised = jnp.exp(logits - jnp.max(logits, axis=1, keepdims=True))
    combine = (slot_raised / jnp.sum(slot_raised, axis=1, keepdims=True)).astype(jnp.bfloat16)
    arrived = lax.all_to_all(slot_in, ("dp", "expert"), split_axis=1, concat_axis=0, tiled=True)
    inner = jnp.einsum("rkd,kdh->rkh", arrived, expert_in, preferred_element_type=jnp.float32)
    inner = jax.nn.gelu(inner, approximate=False).astype(jnp.bfloat16)
    produced = jnp.einsum(
        "rkh,khd->rkd", inner, expert_out, preferred_element_type=jnp.float32
    ).astype(jnp.bfloat16)
    returned = lax.all_to_all(produced, ("dp", "expert"), split_axis=0, concat_axis=1, tiled=True)
    masked_combine = jnp.where(member[:, :, None], combine[None], jnp.zeros((), jnp.bfloat16))
    mixture = jnp.einsum(
        "ste,sed->td", masked_combine, returned, preferred_element_type=jnp.float32
    )
    return (hidden.astype(jnp.float32) + mixture).astype(jnp.bfloat16)


def solution(mesh):
    in_specs = (
        P(("dp", "expert"), None),
        P(("dp", "expert")),
        P(("dp", "expert")),
        P(("dp", "expert"), None),
        P(),
        P(),
        P(),
        P(("dp", "expert"), None, None),
        P(("dp", "expert"), None, None),
    )
    out_specs = P(("dp", "expert"), None)
    return jax.shard_map(
        per_device, mesh=mesh, in_specs=in_specs, out_specs=out_specs, check_vma=False
    )
```

profile of v0, /device:TPU:0, one launch (start us, length us, event | category | flops | bytes accessed | tf_op | source)
XLA Modules:
  0.0 129.7 jit_solution(2665563277811735004)
XLA Ops:
  0.0 0.0 copy-start
  0.0 0.8 fusion.97
  0.8 0.1 fusion.94
  0.9 0.2 select_reduce_fusion.2
  1.1 0.1 select_reduce_fusion.1
  1.3 0.7 copy.42
  1.9 4.3 %all-to-all-start = ((s32[4,1,1]{2,1,0:T(1,128)}), s32[4,1,1]{2,1,0:T(1,128)S(1)}, u32[]{:S(2)}, u32[]{:S(2)}) async-start(s32[4,1,1]{2,1,0:T(1,128)} %copy.42), calls=%async_computation | async-start | bytes 4096 | tf_op jit(solution)/shard_map/all_to_all | solution.py:60
  6.2 2.6 %reshape.151 = bf16[4,98304]{1,0:T(4,128)(2,1)} reshape(bf16[512,768]{1,0:T(8,128)(2,1)} %param.9) | data formatting | bytes 1572864 | tf_op jit(solution)/shard_map/reshape | solution.py:47
  8.8 2.6 %fusion.2 = bf16[4,1,98304]{2,0,1:T(4,128)(2,1)} fusion(bf16[4,98304]{1,0:T(4,128)(2,1)} %reshape.151, s32[4]{0:T(128)S(1)} %add.54), kind=kOutput, calls=%fused_computation.4 | convolution fusion | flops 3538960 | bytes 1572880 | tf_op jit(solution)/shard_map/dot_general | solution.py:48
  11.4 0.5 broadcast.191
  11.9 3.6 %reduce.2 = bf16[4,98304]{1,0:T(4,128)(2,1)} reduce(bf16[4,1,98304]{2,0,1:T(4,128)(2,1)} %fusion.2, bf16[]{:T(256)} %broadcast.191), dimensions={1}, to_apply=%copy.43.reduce_sub_computation | reduce | bytes 1572866 | tf_op jit(solution)/shard_map/reshape | solution.py:54
  15.5 2.8 %reshape.168 = bf16[4,2,49152]{2,1,0:T(2,128)(2,1)} reshape(bf16[4,98304]{1,0:T(4,128)(2,1)} %reduce.2) | data formatting | bytes 1572864
  18.3 0.0 copy-done.7
  18.3 0.6 copy.45
  18.9 0.0 all-to-all-done
  18.9 4.2 %all-to-all-start.1 = ((bf16[4,2,49152]{2,1,0:T(2,128)(2,1)}), bf16[4,2,49152]{2,1,0:T(2,128)(2,1)}, u32[]{:S(2)}, u32[]{:S(2)}) async-start(bf16[4,2,49152]{2,1,0:T(2,128)(2,1)} %reshape.168), calls=%async_computation.1 | async-start | bytes 1572864 | tf_op jit(solution)/shard_map/all_to_all | solution.py:53
  23.1 0.0 copy-done.6
  23.1 0.9 broadcast_in_dim.61
  24.0 1.0 bitcast_and_fusion
  25.0 0.2 reduce
  25.1 9.6 %all-to-all-done.1 = bf16[4,2,49152]{2,1,0:T(2,128)(2,1)} async-done(((bf16[4,2,49152]{2,1,0:T(2,128)(2,1)}), bf16[4,2,49152]{2,1,0:T(2,128)(2,1)}, u32[]{:S(2)}, u32[]{:S(2)}) %all-to-all-start.1) | async-done | bytes 786464 | tf_op jit(solution)/shard_map/all_to_all | solution.py:53
  34.8 3.7 %reshape.169 = bf16[4,1,98304]{2,1,0:T(2,128)(2,1)} reshape(bf16[4,2,49152]{2,1,0:T(2,128)(2,1)} %all-to-all-done.1) | data formatting | bytes 1572864
  38.5 3.6 %fusion.1 = f32[4,98304]{1,0:T(4,128)} fusion(bf16[4,1,98304]{2,1,0:T(2,128)(2,1)} %reshape.169, s32[4]{0:T(128)S(1)} %reduce), kind=kOutput, calls=%fused_computation.3 | convolution fusion | flops 3932176 | bytes 2359312 | tf_op jit(solution)/shard_map/dot_general | solution.py:67
  42.2 3.7 %reshape.163 = f32[512,768]{1,0:T(8,128)} reshape(f32[4,98304]{1,0:T(4,128)} %fusion.1) | data formatting | bytes 3145728 | tf_op jit(solution)/shard_map/convert_element_type | solution.py:91
  45.8 1.6 %reduce_sum.74 = f32[512]{0:T(512)S(1)} reduce(f32[512,768]{1,0:T(8,128)} %reshape.163, f32[]{:T(128)} %constant.50.clone.1), dimensions={1}, to_apply=%region_3.4 | reduce | flops 392704 | bytes 1574916 | tf_op jit(solution)/shard_map/reduce_sum | solution.py:14
  47.4 1.8 %multiply_reduce_fusion = f32[512]{0:T(512)S(1)} fusion(f32[512,768]{1,0:T(8,128)} %reshape.163, f32[512]{0:T(512)S(1)} %broadcast_multiply_fusion.1), kind=kLoop, calls=%fused_computation.46 | loop fusion | flops 1179136 | bytes 1576960 | tf_op jit(solution)/shard_map/reduce_sum | solution.py:15
  49.3 0.0 copy-done
  49.3 0.0 copy-done.1
  49.3 2.1 %convolution_convert_fusion.2 = bf16[512,2304]{1,0:T(8,128)(2,1)S(1)} fusion(bf16[768,2304]{1,0:T(8,128)(2,1)S(1)} %copy-done, f32[512,768]{1,0:T(8,128)S(1)} %copy-done.1, f32[512]{0:T(512)S(1)} %add_rsqrt_fusion.1, f32[512]{0:T(512)S(1)} %broadcast_multiply_fusion.1), kind=kOutput, calls=%fused_computation.17 | convolution fusion | flops 1814298624 | bytes 7475200 | tf_op jit(solution)/shard_map/dot_general | solution.py:74
  51.4 1.5 %fusion.133 = (bf16[512,768]{1,0:T(8,128)(2,1)}, bf16[512,768]{1,0:T(8,128)(2,1)}, bf16[512,768]{1,0:T(8,128)(2,1)}) fusion(bf16[512,2304]{1,0:T(8,128)(2,1)S(1)} %convolution_convert_fusion.2), kind=kLoop, calls=%fused_computation.172 | loop fusion | bytes 4718592 | tf_op jit(solution)/shard_map/slice | solution.py:76
  52.8 2.3 %copy.44 = bf16[512,768]{0,1:T(8,128)(2,1)} copy(bf16[512,768]{1,0:T(8,128)(2,1)} %get-tuple-element.7) | data formatting | bytes 1572864 | tf_op jit(solution)/shard_map/slice | solution.py:77
  55.1 2.3 %copy.46 = bf16[512,768]{0,1:T(8,128)(2,1)} copy(bf16[512,768]{1,0:T(8,128)(2,1)} %get-tuple-element.6) | data formatting | bytes 1572864 | tf_op jit(solution)/shard_map/slice | solution.py:75
  57.4 2.3 %copy.47 = bf16[512,768]{0,1:T(8,128)(2,1)} copy(bf16[512,768]{1,0:T(8,128)(2,1)} %get-tuple-element.5) | data formatting | bytes 1572864 | tf_op jit(solution)/shard_map/slice | solution.py:76
  59.7 11.2 %fusion.134 = (f32[12,512]{1,0:T(8,128)}, f32[12,512,512]{1,2,0:T(8,128)}) fusion(pred[512,512]{0,1:T(8,128)(4,1)} %bitcast_and_fusion, bf16[512,12,64]{0,2,1:T(8,128)(2,1)} %bitcast.139, bf16[512,12,64]{0,2,1:T(8,128)(2,1)} %bitcast.140), kind=kOutput, calls=%fused_computation.173 | convolution fusion | flops 415236608 | bytes 14442496 | tf_op jit(solution)/shard_map/sub | solution.py:86
  70.9 6.1 %fusion.31 = bf16[12,64,512]{2,1,0:T(8,128)(2,1)S(1)} fusion(bf16[512,12,64]{0,2,1:T(8,128)(2,1)} %bitcast.138, f32[12,512,512]{1,2,0:T(8,128)} %get-tuple-element.11, f32[12,512]{1,0:T(8,128)} %get-tuple-element.10), kind=kOutput, calls=%fused_computation.49 | convolution fusion | flops 409337856 | bytes 14180352 | tf_op jit(solution)/shard_map/hqk,khd->qhd/dot_general | solution.py:88
  77.0 0.0 copy-done.2
  77.0 0.0 copy-done.8
  77.0 0.9 convert_reduce_fusion
  78.0 0.0 copy-start.5
  78.0 0.4 fusion.14
  78.4 0.3 fusion.15
  78.6 0.2 copy-done.5
  78.8 0.3 fusion.135
  79.2 0.0 copy-done.3
  79.2 0.0 copy-start.4
  79.2 0.1 select_reduce_fusion
  79.3 0.2 fusion.40
  79.5 0.1 fusion.132
  79.7 0.3 fusion.41
  79.9 0.3 convolution_convert_fusion.3
  80.2 0.4 copy.49
  80.6 13.5 %all_to_all.44 = bf16[4,32,768]{2,0,1:T(4,128)(2,1)} all-to-all(bf16[4,32,768]{2,0,1:T(4,128)(2,1)S(1)} %copy.49), channel_id=1, replica_groups=mesh['dp'=4,'expert'=8] {'dp','expert'}, dimensions={1} | all-to-all | bytes 393216 | tf_op jit(solution)/shard_map/all_to_all | solution.py:111
  94.1 1.7 %reshape.159 = bf16[128,768]{1,0:T(8,128)(2,1)} reshape(bf16[32,4,1,768]{3,1,0,2:T(4,128)(2,1)} %bitcast.141) | data formatting | bytes 393216 | tf_op jit(solution)/shard_map/reshape.1
  95.8 9.2 %fusion.37 = bf16[128,1,768]{2,0,1:T(8,128)(2,1)} fusion(bf16[1,3072,768]{2,1,0:T(8,128)(2,1)} %param.17, bf16[128,768]{1,0:T(8,128)(2,1)} %reshape.159, bf16[1,768,3072]{2,1,0:T(8,128)(2,1)} %param.16), kind=kOutput, calls=%fused_computation.53 | convolution fusion | flops 1233616896 | bytes 9830400 | tf_op jit(solution)/shard_map/rkh,khd->rkd/dot_general | solution.py:114
  104.9 2.2 %reduce.3 = bf16[128,768]{1,0:T(8,128)(2,1)} reduce(bf16[128,1,768]{2,0,1:T(8,128)(2,1)} %fusion.37, bf16[]{:T(256)} %broadcast.191), dimensions={1}, to_apply=%copy.50.reduce_sub_computation | reduce | bytes 393218 | tf_op jit(solution)/shard_map/convert_element_type | solution.py:116
  107.2 1.7 %reshape.170 = bf16[32,2,1536]{2,1,0:T(2,128)(2,1)} reshape(bf16[128,768]{1,0:T(8,128)(2,1)} %reduce.3) | data formatting | bytes 393216
  108.9 3.4 %all-to-all-start.3 = ((bf16[32,2,1536]{2,1,0:T(2,128)(2,1)}), bf16[32,2,1536]{2,1,0:T(2,128)(2,1)}, u32[]{:S(2)}, u32[]{:S(2)}) async-start(bf16[32,2,1536]{2,1,0:T(2,128)(2,1)} %reshape.170), calls=%async_computation.3 | async-start | bytes 393216 | tf_op jit(solution)/shard_map/all_to_all | solution.py:117
  112.3 0.9 fusion.92
  113.2 1.5 %divide_convert_fusion.4 = bf16[512,32]{0,1:T(8,128)(2,1)} fusion(f32[512,32]{0,1:T(8,128)} %copy-done.4, f32[512]{0:T(512)S(1)} %fusion.92, f32[512]{0:T(512)S(1)} %get-tuple-element.14), kind=kLoop, calls=%fused_computation.105 | loop fusion | flops 49152 | bytes 102400 | tf_op jit(solution)/shard_map/convert_element_type | solution.py:110
  114.6 5.9 %all-to-all-done.3 = bf16[32,2,1536]{2,1,0:T(2,128)(2,1)} async-done(((bf16[32,2,1536]{2,1,0:T(2,128)(2,1)}), bf16[32,2,1536]{2,1,0:T(2,128)(2,1)}, u32[]{:S(2)}, u32[]{:S(2)}) %all-to-all-start.3) | async-done | bytes 196640 | tf_op jit(solution)/shard_map/all_to_all | solution.py:117
  120.6 2.2 %reshape.171 = bf16[128,1,768]{2,1,0:T(2,128)(2,1)} reshape(bf16[32,2,1536]{2,1,0:T(2,128)(2,1)} %all-to-all-done.3) | data formatting | bytes 393216
  122.8 2.7 %reduce.1 = bf16[128,768]{1,0:T(8,128)(2,1)} reduce(bf16[128,1,768]{2,1,0:T(2,128)(2,1)} %reshape.171, bf16[]{:T(256)} %constant.140), dimensions={1}, to_apply=%all_to_all.36.reduce_sub_computation | reduce | bytes 393218 | tf_op jit(solution)/shard_map/all_to_all | solution.py:117
  125.5 1.6 %all_to_all.37 = bf16[32,4,1,768]{3,1,0,2:T(4,128)(2,1)} reshape(bf16[128,768]{1,0:T(8,128)(2,1)} %reduce.1) | data formatting | bytes 393216 | tf_op jit(solution)/shard_map/all_to_all | solution.py:117
  127.2 2.5 %fusion.16 = bf16[512,768]{1,0:T(8,128)(2,1)} fusion(bf16[512,768]{1,0:T(8,128)(2,1)} %copy-done.3, bf16[32,4,1,768]{3,1,0,2:T(4,128)(2,1)} %all_to_all.37, pred[4,512]{1,0:T(4,128)(4,1)S(1)} %iota_compare_fusion, bf16[512,32]{0,1:T(8,128)(2,1)} %divide_convert_fusion.4), kind=kOutput, calls=%fused_computation.26 | convolution fusion | flops 101908480 | bytes 1804288 | tf_op jit(solution)/shard_map/ste,sed->td/dot_general | solution.py:119
  (17 shorter events, 0.1 us)
Async XLA Ops:
  0.0 49.3 %copy-start = (bf16[768,2304]{1,0:T(8,128)(2,1)S(1)}, bf16[768,2304]{1,0:T(8,128)(2,1)}, u32[]{:S(2)}) copy-start(bf16[768,2304]{1,0:T(8,128)(2,1)} %param.13) | copy-start | bytes 10616836
  1.9 17.0 %all-to-all-start = ((s32[4,1,1]{2,1,0:T(1,128)}), s32[4,1,1]{2,1,0:T(1,128)S(1)}, u32[]{:S(2)}, u32[]{:S(2)}) async-start(s32[4,1,1]{2,1,0:T(1,128)} %copy.42), calls=%async_computation | async-start | bytes 4096 | tf_op jit(solution)/shard_map/all_to_all | solution.py:60
  11.9 6.4 %copy-start.7 = (s32[4,4]{1,0:T(4,128)S(1)}, s32[4,4]{1,0:T(4,128)}, u32[]{:S(2)}) copy-start(s32[4,4]{1,0:T(4,128)} %param.12) | copy-start | bytes 196
  15.4 7.6 %copy-start.6 = (s32[512]{0:T(512)S(1)}, s32[512]{0:T(512)}, u32[]{:S(2)}) copy-start(s32[512]{0:T(512)} %param.11) | copy-start | bytes 6148
  18.9 15.9 %all-to-all-start.1 = ((bf16[4,2,49152]{2,1,0:T(2,128)(2,1)}), bf16[4,2,49152]{2,1,0:T(2,128)(2,1)}, u32[]{:S(2)}, u32[]{:S(2)}) async-start(bf16[4,2,49152]{2,1,0:T(2,128)(2,1)} %reshape.168), calls=%async_computation.1 | async-start | bytes 1572864 | tf_op jit(solution)/shard_map/all_to_all | solution.py:53
  47.4 1.9 %copy-start.1 = (f32[512,768]{1,0:T(8,128)S(1)}, f32[512,768]{1,0:T(8,128)}, u32[]{:S(2)}) copy-start(f32[512,768]{1,0:T(8,128)} %reshape.163) | copy-start | bytes 4718596
  70.9 6.1 %copy-start.2 = (f32[512,768]{1,0:T(8,128)S(1)}, f32[512,768]{1,0:T(8,128)}, u32[]{:S(2)}) copy-start(f32[512,768]{1,0:T(8,128)} %reshape.163) | copy-start | bytes 4718596
  70.9 6.1 %copy-start.8 = (bf16[768,768]{1,0:T(8,128)(2,1)S(1)}, bf16[768,768]{1,0:T(8,128)(2,1)}, u32[]{:S(2)}) copy-start(bf16[768,768]{1,0:T(8,128)(2,1)} %param.14) | copy-start | bytes 3538948
  78.0 1.2 copy-start.3
  78.0 0.8 copy-start.5
  79.2 1.0 copy-start.4
  108.9 11.7 %all-to-all-start.3 = ((bf16[32,2,1536]{2,1,0:T(2,128)(2,1)}), bf16[32,2,1536]{2,1,0:T(2,128)(2,1)}, u32[]{:S(2)}, u32[]{:S(2)}) async-start(bf16[32,2,1536]{2,1,0:T(2,128)(2,1)} %reshape.170), calls=%async_computation.3 | async-start | bytes 393216 | tf_op jit(solution)/shard_map/all_to_all | solution.py:117
where the time goes:
time: 131 us; the launch traced here: 130 us
  matrix products  39.4 us (30%)
  local copies, waits for them, and re-layouts  31.7 us (24%)
  other arithmetic  17.4 us (13%)
  waiting for transfers between devices  15.6 us (12%)
  blocking collectives  13.5 us (10%)
  starting transfers between devices  11.9 us (9%)
    all_to_all x1, blocking collectives, per_device(): lax.all_to_all(slot_in, ('dp', 'expert'), split_axis=1, concat_axis=0, ti...  13.5 us
    sub x1, matrix products, per_device(): raised = jnp.exp(scores - jnp.max(scores, axis=2, keepdims=True))  11.2 us
    unnamed x22, local copies, waits for them, and re-layouts  10.7 us
    all_to_all x1, waiting for transfers between devices, per_device(): lax.all_to_all(send_rows.reshape(data_count, peer_cap, block_rows * width...  9.65 us
    dot_general x1, matrix products, per_device(): jnp.einsum('rkh,khd->rkd', inner, expert_out, preferred_element_type=jnp....  9.17 us
    dot_general x1, matrix products, per_device(): jnp.einsum('hqk,khd->qhd', weights, value_rows, preferred_element_type=jn...  6.08 us
    all_to_all x1, waiting for transfers between devices, per_device(): lax.all_to_all(produced, ('dp', 'expert'), split_axis=0, concat_axis=1, t...  5.92 us
    all_to_all x1, starting transfers between devices, per_device(): lax.all_to_all(send_place.reshape(data_count, peer_cap), 'dp', split_axis...  4.26 us
  transfers between devices with their start and end apart: 3, of which 2 were waited for; matrix products, arithmetic and copies ran while one was open for 13% of the time, Pallas kernels for 0%

commit v1 on v0

--- a/solution.py
+++ b/solution.py
@@ -114,7 +114,10 @@
     produced = jnp.einsum(
         "rkh,khd->rkd", inner, expert_out, preferred_element_type=jnp.float32
     ).astype(jnp.bfloat16)
-    returned = lax.all_to_all(produced, ("dp", "expert"), split_axis=0, concat_axis=1, tiled=True)
+    size = lax.axis_size(("dp", "expert"))
+    blocks = jnp.stack(jnp.split(produced, size, axis=0), axis=0)
+    blocks = lax.all_to_all(blocks, ("dp", "expert"), split_axis=0, concat_axis=0)
+    returned = jnp.concatenate(blocks, axis=1)
     masked_combine = jnp.where(member[:, :, None], combine[None], jnp.zeros((), jnp.bfloat16))
     mixture = jnp.einsum(
         "ste,sed->td", masked_combine, returned, preferred_element_type=jnp.float32

time: 131 us -> 164 us (1.25); the launches traced: 130 us -> 161 us
  local copies, waits for them, and re-layouts: 31.7 us -> 67.8 us
  other arithmetic: 17.4 us -> 12.4 us
    unnamed x22 -> x51, local copies, waits for them, and re-layouts: 10.7 us -> 47.2 us
    all_to_all x1 -> x0, other arithmetic: 2.74 us -> none  [per_device(): lax.all_to_all(produced, ('dp', 'expert'), split_axis=0, concat_axis=1, t...]
    convert_element_type x1 -> x0, other arithmetic: 2.25 us -> none  [per_device(): produced = jnp.einsum('rkh,khd->rkd', inner, expert_out, preferred_elemen...]
    all_to_all x1 -> x0, local copies, waits for them, and re-layouts: 1.65 us -> none  [per_device(): lax.all_to_all(produced, ('dp', 'expert'), split_axis=0, concat_axis=1, t...]
  transfers between devices with their start and end apart: 3 -> 3, of which waited for: 2 -> 2; matrix products, arithmetic and copies ran while one was open for 13% -> 11% of each run, Pallas kernels for 0% -> 0%
where the time goes in v1:
time: 164 us; the launch traced here: 161 us
  local copies, waits for them, and re-layouts  67.8 us (41%)
  matrix products  39.4 us (24%)
  waiting for transfers between devices  15.6 us (10%)
  blocking collectives  13.5 us (8%)
  other arithmetic  12.4 us (8%)
  starting transfers between devices  11.9 us (7%)
    unnamed x51, local copies, waits for them, and re-layouts  47.2 us
    all_to_all x1, blocking collectives, per_device(): lax.all_to_all(slot_in, ('dp', 'expert'), split_axis=1, concat_axis=0, ti...  13.5 us
    sub x1, matrix products, per_device(): raised = jnp.exp(scores - jnp.max(scores, axis=2, keepdims=True))  11.2 us
    all_to_all x1, waiting for transfers between devices, per_device(): lax.all_to_all(send_rows.reshape(data_count, peer_cap, block_rows * width...  9.65 us
    dot_general x1, matrix products, per_device(): jnp.einsum('rkh,khd->rkd', inner, expert_out, preferred_element_type=jnp....  9.17 us
    dot_general x1, matrix products, per_device(): jnp.einsum('hqk,khd->qhd', weights, value_rows, preferred_element_type=jn...  6.08 us
    all_to_all x1, waiting for transfers between devices, per_device(): lax.all_to_all(blocks, ('dp', 'expert'), split_axis=0, concat_axis=0)  5.92 us
    all_to_all x1, starting transfers between devices, per_device(): lax.all_to_all(send_place.reshape(data_count, peer_cap), 'dp', split_axis...  4.26 us
  transfers between devices with their start and end apart: 3, of which 2 were waited for; matrix products, arithmetic and copies ran while one was open for 11% of the time, Pallas kernels for 0%

profile of v1, /device:TPU:0, one launch (start us, length us, event | category | flops | bytes accessed | tf_op | source)
XLA Modules:
  0.0 160.8 jit_solution(4542092990415758179)
XLA Ops:
  0.0 0.8 fusion.96
  1.3 0.7 copy.41
  1.9 4.3 %all-to-all-start = ((s32[4,1,1]{2,1,0:T(1,128)}), s32[4,1,1]{2,1,0:T(1,128)S(1)}, u32[]{:S(2)}, u32[]{:S(2)}) async-start(s32[4,1,1]{2,1,0:T(1,128)} %copy.41), calls=%async_computation | async-start | bytes 4096 | tf_op jit(solution)/shard_map/all_to_all | solution.py:60
  6.2 2.6 %reshape.157 = bf16[4,98304]{1,0:T(4,128)(2,1)} reshape(bf16[512,768]{1,0:T(8,128)(2,1)} %param.9) | data formatting | bytes 1572864 | tf_op jit(solution)/shard_map/reshape | solution.py:47
  8.8 2.6 %fusion.2 = bf16[4,1,98304]{2,0,1:T(4,128)(2,1)} fusion(bf16[4,98304]{1,0:T(4,128)(2,1)} %reshape.157, s32[4]{0:T(128)S(1)} %add.54), kind=kOutput, calls=%fused_computation.4 | convolution fusion | flops 3538960 | bytes 1572880 | tf_op jit(solution)/shard_map/dot_general | solution.py:48
  11.9 3.5 %reduce.1 = bf16[4,98304]{1,0:T(4,128)(2,1)} reduce(bf16[4,1,98304]{2,0,1:T(4,128)(2,1)} %fusion.2, bf16[]{:T(256)} %broadcast.190), dimensions={1}, to_apply=%copy.42.reduce_sub_computation | reduce | bytes 1572866 | tf_op jit(solution)/shard_map/reshape | solution.py:54
  15.4 2.8 %reshape.175 = bf16[4,2,49152]{2,1,0:T(2,128)(2,1)} reshape(bf16[4,98304]{1,0:T(4,128)(2,1)} %reduce.1) | data formatting | bytes 1572864
  18.9 4.2 %all-to-all-start.1 = ((bf16[4,2,49152]{2,1,0:T(2,128)(2,1)}), bf16[4,2,49152]{2,1,0:T(2,128)(2,1)}, u32[]{:S(2)}, u32[]{:S(2)}) async-start(bf16[4,2,49152]{2,1,0:T(2,128)(2,1)} %reshape.175), calls=%async_computation.1 | async-start | bytes 1572864 | tf_op jit(solution)/shard_map/all_to_all | solution.py:53
  23.1 0.9 broadcast_in_dim.61
  24.0 1.0 bitcast_and_fusion
  25.1 9.6 %all-to-all-done.1 = bf16[4,2,49152]{2,1,0:T(2,128)(2,1)} async-done(((bf16[4,2,49152]{2,1,0:T(2,128)(2,1)}), bf16[4,2,49152]{2,1,0:T(2,128)(2,1)}, u32[]{:S(2)}, u32[]{:S(2)}) %all-to-all-start.1) | async-done | bytes 786464 | tf_op jit(solution)/shard_map/all_to_all | solution.py:53
  34.8 3.7 %reshape.176 = bf16[4,1,98304]{2,1,0:T(2,128)(2,1)} reshape(bf16[4,2,49152]{2,1,0:T(2,128)(2,1)} %all-to-all-done.1) | data formatting | bytes 1572864
  38.5 3.6 %fusion.1 = f32[4,98304]{1,0:T(4,128)} fusion(bf16[4,1,98304]{2,1,0:T(2,128)(2,1)} %reshape.176, s32[4]{0:T(128)S(1)} %reduce), kind=kOutput, calls=%fused_computation.3 | convolution fusion | flops 3932176 | bytes 2359312 | tf_op jit(solution)/shard_map/dot_general | solution.py:67
  42.1 3.7 %reshape.171 = f32[512,768]{1,0:T(8,128)} reshape(f32[4,98304]{1,0:T(4,128)} %fusion.1) | data formatting | bytes 3145728 | tf_op jit(solution)/shard_map/convert_element_type | solution.py:91
  45.8 1.6 reduce_sum.74
  47.4 1.8 %multiply_reduce_fusion = f32[512]{0:T(512)S(1)} fusion(f32[512,768]{1,0:T(8,128)} %reshape.171, f32[512]{0:T(512)S(1)} %broadcast_multiply_fusion.1), kind=kLoop, calls=%fused_computation.46 | loop fusion | flops 1179136 | bytes 1576960 | tf_op jit(solution)/shard_map/reduce_sum | solution.py:15
  49.2 2.1 %convolution_convert_fusion.2 = bf16[512,2304]{1,0:T(8,128)(2,1)S(1)} fusion(bf16[768,2304]{1,0:T(8,128)(2,1)S(1)} %copy-done, f32[512,768]{1,0:T(8,128)S(1)} %copy-done.1, f32[512]{0:T(512)S(1)} %add_rsqrt_fusion.1, f32[512]{0:T(512)S(1)} %broadcast_multiply_fusion.1), kind=kOutput, calls=%fused_computation.17 | convolution fusion | flops 1814298624 | bytes 7475200 | tf_op jit(solution)/shard_map/dot_general | solution.py:74
  51.3 1.5 fusion.132
  52.8 2.3 %copy.43 = bf16[512,768]{0,1:T(8,128)(2,1)} copy(bf16[512,768]{1,0:T(8,128)(2,1)} %get-tuple-element.7) | data formatting | bytes 1572864 | tf_op jit(solution)/shard_map/slice | solution.py:77
  55.1 2.3 %copy.45 = bf16[512,768]{0,1:T(8,128)(2,1)} copy(bf16[512,768]{1,0:T(8,128)(2,1)} %get-tuple-element.6) | data formatting | bytes 1572864 | tf_op jit(solution)/shard_map/slice | solution.py:75
  57.4 2.3 %copy.46 = bf16[512,768]{0,1:T(8,128)(2,1)} copy(bf16[512,768]{1,0:T(8,128)(2,1)} %get-tuple-element.5) | data formatting | bytes 1572864 | tf_op jit(solution)/shard_map/slice | solution.py:76
  59.7 11.2 %fusion.133 = (f32[12,512]{1,0:T(8,128)}, f32[12,512,512]{1,2,0:T(8,128)}) fusion(pred[512,512]{0,1:T(8,128)(4,1)} %bitcast_and_fusion, bf16[512,12,64]{0,2,1:T(8,128)(2,1)} %bitcast.265, bf16[512,12,64]{0,2,1:T(8,128)(2,1)} %bitcast.266), kind=kOutput, calls=%fused_computation.236 | convolution fusion | flops 415236608 | bytes 14442496 | tf_op jit(solution)/shard_map/sub | solution.py:86
  70.9 6.1 %fusion.31 = bf16[12,64,512]{2,1,0:T(8,128)(2,1)S(1)} fusion(bf16[512,12,64]{0,2,1:T(8,128)(2,1)} %bitcast.264, f32[12,512,512]{1,2,0:T(8,128)} %get-tuple-element.11, f32[12,512]{1,0:T(8,128)} %get-tuple-element.10), kind=kOutput, calls=%fused_computation.49 | convolution fusion | flops 409337856 | bytes 14180352 | tf_op jit(solution)/shard_map/hqk,khd->qhd/dot_general | solution.py:88
  77.0 0.9 convert_reduce_fusion
  80.5 13.5 %all_to_all.31 = bf16[4,32,768]{2,0,1:T(4,128)(2,1)} all-to-all(bf16[4,32,768]{2,0,1:T(4,128)(2,1)S(1)} %copy.48), channel_id=1, replica_groups=mesh['dp'=4,'expert'=8] {'dp','expert'}, dimensions={1} | all-to-all | bytes 393216 | tf_op jit(solution)/shard_map/all_to_all | solution.py:111
  94.1 1.7 %reshape.165 = bf16[128,768]{1,0:T(8,128)(2,1)} reshape(bf16[32,4,1,768]{3,1,0,2:T(4,128)(2,1)} %bitcast.267) | data formatting | bytes 393216 | tf_op jit(solution)/shard_map/reshape.1
  95.7 9.2 %fusion.37 = bf16[128,1,768]{2,0,1:T(8,128)(2,1)} fusion(bf16[1,3072,768]{2,1,0:T(8,128)(2,1)} %param.17, bf16[128,768]{1,0:T(8,128)(2,1)} %reshape.165, bf16[1,768,3072]{2,1,0:T(8,128)(2,1)} %param.16), kind=kOutput, calls=%fused_computation.53 | convolution fusion | flops 1233616896 | bytes 9830400 | tf_op jit(solution)/shard_map/rkh,khd->rkd/dot_general | solution.py:114
  104.9 1.3 constant_dynamic-update-slice_fusion.31
  106.2 1.3 constant_dynamic-update-slice_fusion.30
  107.5 1.3 constant_dynamic-update-slice_fusion.29
  108.8 1.3 constant_dynamic-update-slice_fusion.28
  110.1 1.3 constant_dynamic-update-slice_fusion.27
  111.4 1.3 constant_dynamic-update-slice_fusion.26
  112.7 1.3 constant_dynamic-update-slice_fusion.25
  114.0 1.3 constant_dynamic-update-slice_fusion.24
  115.3 1.3 constant_dynamic-update-slice_fusion.23
  116.6 1.3 constant_dynamic-update-slice_fusion.22
  117.9 1.3 constant_dynamic-update-slice_fusion.21
  119.2 1.3 constant_dynamic-update-slice_fusion.20
  120.5 1.3 constant_dynamic-update-slice_fusion.19
  121.8 1.3 constant_dynamic-update-slice_fusion.18
  123.1 1.3 constant_dynamic-update-slice_fusion.17
  124.4 1.3 constant_dynamic-update-slice_fusion.16
  125.7 1.3 constant_dynamic-update-slice_fusion.15
  127.0 1.3 constant_dynamic-update-slice_fusion.14
  128.3 1.3 constant_dynamic-update-slice_fusion.13
  129.6 1.3 constant_dynamic-update-slice_fusion.12
  130.9 1.3 constant_dynamic-update-slice_fusion.11
  132.2 1.3 constant_dynamic-update-slice_fusion.10
  133.6 1.3 constant_dynamic-update-slice_fusion.9
  134.9 1.3 constant_dynamic-update-slice_fusion.8
  136.2 1.3 constant_dynamic-update-slice_fusion.7
  137.5 1.3 constant_dynamic-update-slice_fusion.6
  138.8 1.3 constant_dynamic-update-slice_fusion.5
  140.1 1.3 constant_dynamic-update-slice_fusion.4
  141.4 1.3 constant_dynamic-update-slice_fusion.3
  142.7 1.3 constant_dynamic-update-slice_fusion.2
  144.0 1.3 constant_dynamic-update-slice_fusion.1
  145.3 1.3 constant_dynamic-update-slice_fusion
  146.6 3.4 %all-to-all-start.3 = ((bf16[32,4,1,768]{3,1,2,0:T(4,128)(2,1)}), bf16[32,4,1,768]{3,1,2,0:T(4,128)(2,1)}, u32[]{:S(2)}, u32[]{:S(2)}) async-start(bf16[32,4,1,768]{3,1,2,0:T(4,128)(2,1)} %constant_dynamic-update-slice_fusion), calls=%async_computation.3 | async-start | bytes 393216 | tf_op jit(solution)/shard_map/all_to_all | solution.py:119
  150.0 0.9 fusion.91
  150.9 1.5 divide_convert_fusion.4
  152.3 5.9 %all-to-all-done.3 = bf16[32,4,1,768]{3,1,2,0:T(4,128)(2,1)} async-done(((bf16[32,4,1,768]{3,1,2,0:T(4,128)(2,1)}), bf16[32,4,1,768]{3,1,2,0:T(4,128)(2,1)}, u32[]{:S(2)}, u32[]{:S(2)}) %all-to-all-start.3) | async-done | bytes 196640 | tf_op jit(solution)/shard_map/all_to_all | solution.py:119
  158.3 2.5 %fusion.16 = bf16[512,768]{1,0:T(8,128)(2,1)} fusion(bf16[512,768]{1,0:T(8,128)(2,1)} %copy-done.3, bf16[4,32,768]{2,0,1:T(4,128)(2,1)} %bitcast.59, pred[4,512]{1,0:T(4,128)(4,1)S(1)} %iota_compare_fusion, bf16[512,32]{0,1:T(8,128)(2,1)} %divide_convert_fusion.4), kind=kOutput, calls=%fused_computation.26 | convolution fusion | flops 101908480 | bytes 1804288 | tf_op jit(solution)/shard_map/ste,sed->td/dot_general | solution.py:122
  (44 shorter events, 4.3 us)
Async XLA Ops:
  0.0 49.2 %copy-start = (bf16[768,2304]{1,0:T(8,128)(2,1)S(1)}, bf16[768,2304]{1,0:T(8,128)(2,1)}, u32[]{:S(2)}) copy-start(bf16[768,2304]{1,0:T(8,128)(2,1)} %param.13) | copy-start | bytes 10616836
  1.9 16.9 %all-to-all-start = ((s32[4,1,1]{2,1,0:T(1,128)}), s32[4,1,1]{2,1,0:T(1,128)S(1)}, u32[]{:S(2)}, u32[]{:S(2)}) async-start(s32[4,1,1]{2,1,0:T(1,128)} %copy.41), calls=%async_computation | async-start | bytes 4096 | tf_op jit(solution)/shard_map/all_to_all | solution.py:60
  11.9 6.4 %copy-start.7 = (s32[4,4]{1,0:T(4,128)S(1)}, s32[4,4]{1,0:T(4,128)}, u32[]{:S(2)}) copy-start(s32[4,4]{1,0:T(4,128)} %param.12) | copy-start | bytes 196
  15.4 7.6 %copy-start.6 = (s32[512]{0:T(512)S(1)}, s32[512]{0:T(512)}, u32[]{:S(2)}) copy-start(s32[512]{0:T(512)} %param.11) | copy-start | bytes 6148
  18.9 15.9 %all-to-all-start.1 = ((bf16[4,2,49152]{2,1,0:T(2,128)(2,1)}), bf16[4,2,49152]{2,1,0:T(2,128)(2,1)}, u32[]{:S(2)}, u32[]{:S(2)}) async-start(bf16[4,2,49152]{2,1,0:T(2,128)(2,1)} %reshape.175), calls=%async_computation.1 | async-start | bytes 1572864 | tf_op jit(solution)/shard_map/all_to_all | solution.py:53
  47.4 1.9 %copy-start.1 = (f32[512,768]{1,0:T(8,128)S(1)}, f32[512,768]{1,0:T(8,128)}, u32[]{:S(2)}) copy-start(f32[512,768]{1,0:T(8,128)} %reshape.171) | copy-start | bytes 4718596
  70.9 6.1 %copy-start.2 = (f32[512,768]{1,0:T(8,128)S(1)}, f32[512,768]{1,0:T(8,128)}, u32[]{:S(2)}) copy-start(f32[512,768]{1,0:T(8,128)} %reshape.171) | copy-start | bytes 4718596
  70.9 6.1 %copy-start.8 = (bf16[768,768]{1,0:T(8,128)(2,1)S(1)}, bf16[768,768]{1,0:T(8,128)(2,1)}, u32[]{:S(2)}) copy-start(bf16[768,768]{1,0:T(8,128)(2,1)} %param.14) | copy-start | bytes 3538948
  77.9 1.2 copy-start.3
  77.9 0.8 copy-start.5
  79.1 1.0 copy-start.4
  146.6 11.7 %all-to-all-start.3 = ((bf16[32,4,1,768]{3,1,2,0:T(4,128)(2,1)}), bf16[32,4,1,768]{3,1,2,0:T(4,128)(2,1)}, u32[]{:S(2)}, u32[]{:S(2)}) async-start(bf16[32,4,1,768]{3,1,2,0:T(4,128)(2,1)} %constant_dynamic-update-slice_fusion), calls=%async_computation.3 | async-start | bytes 393216 | tf_op jit(solution)/shard_map/all_to_all | solution.py:119
